TPU v7x, 512 devices: a whole 4x4x16 slice. The times are simulated.
512 devices in a mesh: blk: 32 (over y, z_lo, core), rep: 16 (over x, z_hi).
Axes of the slice: x: 4, y: 4, z: 16 (z_hi: 4, z_lo: 4; z = z_hi * 4 + z_lo), core: 2. Of those that a mesh axis runs over, the one named last changes fastest.
Arguments:
- point_pool: bfloat16 [655360, 1024], P(('blk', 'rep')), may hold values from -8 to 8
- batch_rows: int32 [524288], P(('blk', 'rep')), may hold values from 0 to 1279
- targets: bfloat16 [524288, 256], P(('blk', 'rep')), may hold values from -6 to 6
- center_pool: bfloat16 [2048, 1024], P('blk'), may hold values from -8 to 8
- center_rows: int32 [1024], P('blk'), may hold values from 0 to 63
- coefs: bfloat16 [1024, 256], P('blk'), may hold values from -1.5 to 1.5
Outputs:
- residual: float32 [524288, 256], P(('blk', 'rep'))
- coef_grad: float32 [1024, 256], P('blk')
All inputs are finite; a program needn't handle non-finite values.
Results may differ from a plain program's by a relative error of at most 0.0016.
Values may be sent and summed in bfloat16 or wider, within the bound.
A program may use at most 64 MiB of HBM per device.

v0:
```python
import jax
import jax.numpy as jnp
from jax import lax
from jax.sharding import Mesh
from jax.sharding import PartitionSpec as P

BLK = ("blk_0", "blk_1", "blk_2")
BLK_REP = ("blk_0", "blk_1", "blk_2", "rep")


def sent_to_all(x, axis):
    copies = jnp.broadcast_to(x, (lax.axis_size(axis), *x.shape))
    return lax.all_to_all(copies, axis, split_axis=0, concat_axis=0, tiled=True)


def in_order(parts, dim):
    parts = jnp.moveaxis(parts, 0, dim)
    shape = parts.shape
    return parts.reshape(*shape[:dim], shape[dim] * shape[dim + 1], *shape[dim + 2 :])


def gathered_by_axis(x, axes, dim):
    far, near = axes
    parts = sent_to_all(sent_to_all(x, far), near)
    return in_order(parts.swapaxes(0, 1).reshape(-1, *x.shape), dim)


def side_by_side(arrays, axis, dim, along):
    widths = [a.shape[along] for a in arrays]
    both = jnp.concatenate(arrays, axis=along)
    whole = gathered_by_axis(both, axis, dim)
    return tuple(jnp.split(whole, [sum(widths[:k]) for k in range(1, len(widths))], axis=along))


def in_blocks(x, dim, length):
    before, after = (x.shape[:dim], x.shape[dim + 1 :])
    return jnp.moveaxis(x.reshape(*before, length, -1, *after), dim, 0)


def sent_and_summed(x, axis, dim):
    parts = in_blocks(x, dim, lax.axis_size(axis))
    arrived = lax.all_to_all(parts, axis, split_axis=0, concat_axis=0, tiled=True)
    return arrived.sum(axis=0)


def of_everyone(x, axis):
    everything = sent_to_all(x, axis)
    return jnp.sum(everything, axis=0)


def kernel_block(points, point_norm, center_piece):
    center_norm = jnp.sum(center_piece.astype(jnp.float32) ** 2, axis=1)
    inner = lax.dot_general(
        points, center_piece, (((1,), (1,)), ((), ())), preferred_element_type=jnp.float32
    )
    distance = point_norm[:, None] + center_norm[None, :] - 2.0 * inner
    return jnp.exp(-distance / points.shape[1]).astype(jnp.bfloat16)


def transposed_product(kernel, residual_b):
    return lax.dot_general(
        kernel, residual_b, (((0,), (0,)), ((), ())), preferred_element_type=jnp.float32
    )


def per_device(point_pool, batch_rows, targets, center_pool, center_rows, coefs):
    points = jnp.take(point_pool, batch_rows, axis=0)
    centers = jnp.take(center_pool, center_rows, axis=0)
    point_norm = jnp.sum(points.astype(jnp.float32) ** 2, axis=1)
    pieces = side_by_side((centers, coefs), (("blk_0", "blk_1"), "blk_2"), 0, 1)
    kernel = kernel_block(points, point_norm, pieces[0])
    prediction = jnp.dot(kernel, pieces[1], preferred_element_type=jnp.float32)
    residual = prediction - targets.astype(jnp.float32)
    residual_b = residual.astype(jnp.bfloat16)
    partial_grad = sent_and_summed(transposed_product(kernel, residual_b), BLK, 0)
    coef_grad = of_everyone(partial_grad, "rep")
    return (residual, coef_grad)


def solution(mesh):
    finer = Mesh(
        mesh.devices.reshape(4, 4, 2, mesh.shape["rep"]), ("blk_0", "blk_1", "blk_2", "rep")
    )
    in_specs = (P(BLK_REP, None), P(BLK_REP), P(BLK_REP, None), P(BLK, None), P(BLK), P(BLK, None))
    out_specs = (P(BLK_REP, None), P(BLK, None))
    return jax.shard_map(
        per_device, mesh=finer, in_specs=in_specs, out_specs=out_specs, check_vma=False
    )
```

profile of v0, /device:TPU:9, one launch (start us, length us, event | category | flops | bytes accessed | tf_op | source)
XLA Modules:
  0.0 142.4 jit_solution(11102323378973991275)
XLA Ops:
  0.6 0.0 copy-start
  0.6 0.0 copy-start.2
  0.7 0.8 compare_and_fusion.1
  1.5 0.7 compare_select_fusion.1
  2.1 1.6 %gather_fusion.1 = bf16[32,1024]{1,0:T(8,128)(2,1)S(1)} fusion(bf16[64,1024]{1,0:T(8,128)(2,1)} %param.9, s32[1024]{0:T(1024)S(1)} %pad_clamp_fusion), kind=kCustom, calls=%fused_computation.1 | custom fusion | bytes 131200 | tf_op jit(solution)/shard_map/jit(_take)/gather | solution.py:68
  3.7 0.1 broadcast_select_fusion.2
  3.8 0.7 pad_maximum_fusion
  4.5 1.2 broadcast_in_dim.41
  5.7 8.4 %all-to-all-start = ((bf16[16,32,1280]{2,1,0:T(8,128)(2,1)}), bf16[16,32,1280]{2,1,0:T(8,128)(2,1)}, u32[]{:S(2)}, u32[]{:S(2)}) async-start(bf16[16,32,1280]{2,1,0:T(8,128)(2,1)} %broadcast_in_dim.41), calls=%async_computation | async-start | bytes 2621440 | tf_op jit(solution)/shard_map/all_to_all | solution.py:13
  14.2 0.0 copy-done.2
  14.2 0.0 copy-done
  14.2 5.4 %gather_fusion = bf16[1024,1024]{1,0:T(8,128)(2,1)} fusion(bf16[1280,1024]{1,0:T(8,128)(2,1)S(1)} %copy-done, s32[1024]{0:T(1024)S(1)} %fusion.4), kind=kCustom, calls=%fused_computation | custom fusion | bytes 4198400 | tf_op jit(solution)/shard_map/jit(_take)/gather | solution.py:67
  19.6 2.3 %multiply_reduce_fusion.1 = f32[1024]{0:T(1024)S(1)} fusion(bf16[1024,1024]{1,0:T(8,128)(2,1)} %gather_fusion, pred[1024]{0:T(1024)(128)(4,1)S(1)} %compare_and_fusion), kind=kLoop, calls=%fused_computation.4 | loop fusion | flops 4193280 | bytes 2102272 | tf_op jit(solution)/shard_map/reduce_sum | solution.py:69
  21.9 22.7 %all-to-all-done = bf16[16,32,1280]{2,1,0:T(8,128)(2,1)} async-done(((bf16[16,32,1280]{2,1,0:T(8,128)(2,1)}), bf16[16,32,1280]{2,1,0:T(8,128)(2,1)}, u32[]{:S(2)}, u32[]{:S(2)}) %all-to-all-start) | async-done | bytes 1310752 | tf_op jit(solution)/shard_map/all_to_all | solution.py:13
  44.6 1.6 %broadcast_in_dim.42 = bf16[2,16,32,1280]{3,2,1,0:T(8,128)(2,1)S(1)} broadcast(bf16[16,32,1280]{2,1,0:T(8,128)(2,1)} %all-to-all-done), dimensions={1,2,3} | broadcast | bytes 3932160 | tf_op jit(solution)/shard_map/broadcast_in_dim | solution.py:12
  46.2 7.2 %all_to_all.20 = bf16[2,16,32,1280]{3,2,1,0:T(8,128)(2,1)S(1)} all-to-all(bf16[2,16,32,1280]{3,2,1,0:T(8,128)(2,1)S(1)} %broadcast_in_dim.42), channel_id=1, replica_groups=mesh['blk_0'=4,'blk_1'=4,'blk_2'=2,'rep'=16] {'blk_2'}, dimensions={0} | all-to-all | bytes 5242880 | tf_op jit(solution)/shard_map/all_to_all | solution.py:13
  53.4 0.0 copy-start.1
  53.4 0.2 copy.9
  53.6 0.5 multiply_reduce_fusion
  54.1 0.9 copy-done.1
  55.0 0.0 copy-start.3
  55.0 3.1 %exponential_convert_fusion = bf16[1024,1024]{1,0:T(8,128)(2,1)S(1)} fusion(f32[1024]{0:T(1024)S(1)} %multiply_reduce_fusion, f32[1024]{0:T(1024)S(1)} %multiply_reduce_fusion.1, bf16[1024,1280]{1,0:T(8,128)(2,1)S(1)} %bitcast.7, bf16[1024,1024]{1,0:T(8,128)(2,1)S(1)} %copy-done.1, pred[1024]{0:T(1024)(128)(4,1)S(1)} %compare_and_fusion), kind=kOutput, calls=%fused_computation.2 | convolution fusion | flops 2154823680 | bytes 6300672 | tf_op jit(solution)/shard_map/dot_general | solution.py:53
  58.1 0.0 copy-done.3
  58.1 0.7 convolution_subtract_fusion
  58.9 0.0 copy-start.4
  58.9 0.8 fusion.2
  59.6 0.2 copy-done.4
  59.8 33.1 %all_to_all.21 = f32[32,32,256]{2,1,0:T(8,128)} all-to-all(f32[32,32,256]{2,1,0:T(8,128)S(1)} %bitcast.9), channel_id=1, replica_groups=mesh['blk_0'=4,'blk_1'=4,'blk_2'=2,'rep'=16] {'blk_0','blk_1','blk_2'}, dimensions={0} | all-to-all | bytes 2097152 | tf_op jit(solution)/shard_map/all_to_all | solution.py:42
  93.0 1.3 reduce_sum.38
  94.3 47.5 %all_to_all.22 = f32[16,32,256]{2,1,0:T(8,128)S(1)} all-to-all(f32[16,32,256]{2,1,0:T(8,128)S(1)} %broadcast_in_dim.43), channel_id=1, replica_groups=mesh['blk_0'=4,'blk_1'=4,'blk_2'=2,'rep'=16] {'rep'}, dimensions={0} | all-to-all | bytes 1048576 | tf_op jit(solution)/shard_map/all_to_all | solution.py:13
  141.8 0.6 reduce_sum.39
  (4 shorter events, 0.1 us)
Async XLA Ops:
  0.6 13.6 %copy-start = (bf16[1280,1024]{1,0:T(8,128)(2,1)S(1)}, bf16[1280,1024]{1,0:T(8,128)(2,1)}, u32[]{:S(2)}) copy-start(bf16[1280,1024]{1,0:T(8,128)(2,1)} %param.6) | copy-start | bytes 7864324
  0.6 13.5 %copy-start.2 = (s32[1024]{0:T(1024)S(1)}, s32[1024]{0:T(1024)}, u32[]{:S(2)}) copy-start(s32[1024]{0:T(1024)} %param.7) | copy-start | bytes 12292
  5.7 38.9 %all-to-all-start = ((bf16[16,32,1280]{2,1,0:T(8,128)(2,1)}), bf16[16,32,1280]{2,1,0:T(8,128)(2,1)}, u32[]{:S(2)}, u32[]{:S(2)}) async-start(bf16[16,32,1280]{2,1,0:T(8,128)(2,1)} %broadcast_in_dim.41), calls=%async_computation | async-start | bytes 2621440 | tf_op jit(solution)/shard_map/all_to_all | solution.py:13
  53.4 1.6 %copy-start.1 = (bf16[1024,1024]{1,0:T(8,128)(2,1)S(1)}, bf16[1024,1024]{1,0:T(8,128)(2,1)}, u32[]{:S(2)}) copy-start(bf16[1024,1024]{1,0:T(8,128)(2,1)} %gather_fusion) | copy-start | bytes 6291460
  55.0 3.1 %copy-start.3 = (bf16[1024,256]{1,0:T(8,128)(2,1)S(1)}, bf16[1024,256]{1,0:T(8,128)(2,1)}, u32[]{:S(2)}) copy-start(bf16[1024,256]{1,0:T(8,128)(2,1)} %param.8) | copy-start | bytes 1572868
  58.9 1.0 copy-start.4
where the time goes:
time: 143 us; the launch traced here: 142 us
  blocking collectives  87.8 us (61%)
  waiting for transfers between devices  22.7 us (16%)
  local copies, waits for them, and re-layouts  11.1 us (8%)
  starting transfers between devices  8.43 us (6%)
  other arithmetic  7.05 us (5%)
  matrix products  4.61 us (3%)
    all_to_all x2, blocking collectives, sent_to_all(): return lax.all_to_all(copies, axis, split_axis=0, concat_axis=0, tiled=True)  54.6 us
    all_to_all x1, blocking collectives, sent_and_summed(): lax.all_to_all(parts, axis, split_axis=0, concat_axis=0, tiled=True)  33.1 us
    all_to_all x1, waiting for transfers between devices, sent_to_all(): return lax.all_to_all(copies, axis, split_axis=0, concat_axis=0, tiled=True)  22.7 us
    all_to_all x1, starting transfers between devices, sent_to_all(): return lax.all_to_all(copies, axis, split_axis=0, concat_axis=0, tiled=True)  8.43 us
    gather x1, local copies, waits for them, and re-layouts, per_device(): points = jnp.take(point_pool, batch_rows, axis=0)  5.36 us
    dot_general x1, matrix products, kernel_block(): lax.dot_general(points, center_piece, (((1,), (1,)), ((), ())), preferred...  3.12 us
  transfers between devices with their start and end apart: 1, of which 1 were waited for; matrix products, arithmetic and copies ran while one was open for 5% of the time, Pallas kernels for 0%

commit v1 on v0

v1 whole, which is shorter than its diff:
```python
import functools

import jax
import jax.numpy as jnp
from jax import lax
from jax.experimental import pallas as pl
from jax.experimental.pallas import tpu as pltpu
from jax.sharding import PartitionSpec as P

MESH = pl.DeviceIdType.MESH
F32 = jnp.float32
BF16 = jnp.bfloat16
OFFS = (0, 1, -1, 2)
NEG = (0, 2, 1, 3)
NX, NY, NL, NH, NZ = 4, 4, 4, 4, 16


def place():
    b = lax.axis_index("blk")
    r = lax.axis_index("rep")
    core = b % 2
    return (r // NH, b // (2 * NL), (r % NH) * NL + (b // 2) % NL, core)


def at(here, f=0, s=0, x=0, z=0, partner=False):
    px, py, pz, core = here
    nx = (px + x + NX) % NX
    ny = (py + (1 - core) * f + core * s + NY) % NY
    nz = (pz + core * f + (1 - core) * s + z + NZ) % NZ
    nc = 1 - core if partner else core
    return {"blk": (ny * NL + nz % NL) * 2 + nc, "rep": nx * NH + nz // NL}


def fx_offset(i, j):
    df = OFFS[i]
    if df == 2 and j in (1, 2):
        df = -2
    return df, OFFS[j]


def destinations():
    out = [dict(partner=True)]
    for k in (1, -1, 2, -2):
        out += [dict(f=k), dict(s=k)]
    for k in (1, -1, 2):
        out.append(dict(x=k))
    for i in (1, 2, 3):
        for j in (1, 2, 3):
            df, dx = fx_offset(i, j)
            out.append(dict(f=df, x=dx))
    for k in (4, -4, 8):
        out.append(dict(z=k))
    return out


def opposite(offset):
    return {k: (v if k == "partner" else -v) for k, v in offset.items()}


def kernel(
    pool_hbm, rows_ref, targets_hbm, cpool_hbm, crows_ref, coefs_hbm,
    res_hbm, grad_ref,
    cen, pool, sel, pts, pnorm, kern, pred, resb, targ, cpool,
    gq, gq_in, gs, gs_in, gf, gf_in, gz, gz_in, out,
    lsem, send1, send2, send_c, recv_p, recv_q,
    sgq, rgq, sgs, rgs, sgf, rgf, sgz, rgz, sgx, rgx,
):
    here = place()
    npts, d = pts.shape
    npool = pool.shape[0]
    ncen = cen.shape[3]
    outs = pred.shape[1]
    group = 8 * ncen
    half = ncen // 2

    get_cpool = pltpu.make_async_copy(cpool_hbm, cpool, lsem.at[0])
    get_coefs = pltpu.make_async_copy(coefs_hbm, cen.at[0, 0, 0, :, pl.ds(d, outs)], lsem.at[1])
    get_pool = pltpu.make_async_copy(pool_hbm, pool, lsem.at[2])
    get_targ = pltpu.make_async_copy(targets_hbm, targ, lsem.at[3])
    get_cpool.start()
    get_coefs.start()
    get_pool.start()
    get_targ.start()

    barrier = pltpu.get_barrier_semaphore()
    dests = destinations()
    for offset in dests:
        pl.semaphore_signal(barrier, inc=1, device_id=at(here, **opposite(offset)), device_id_type=MESH)

    pending = []

    def send(src, dst, ssem, rsem, **offset):
        copy = pltpu.make_async_remote_copy(
            src_ref=src, dst_ref=dst, send_sem=ssem, recv_sem=rsem,
            device_id=at(here, **offset), device_id_type=MESH,
        )
        copy.start()
        pending.append(copy)

    def arrived(ref, rsem):
        pltpu.make_async_remote_copy(
            src_ref=ref, dst_ref=ref, send_sem=sgx.at[0], recv_sem=rsem,
            device_id=at(here, partner=True), device_id_type=MESH,
        ).wait_recv()

    get_cpool.wait()
    chosen = (
        lax.broadcasted_iota(jnp.int32, (cpool.shape[0], ncen), 0) == crows_ref[...]
    ).astype(F32).astype(BF16)
    cen[0, 0, 0, :, 0:d] = lax.dot_general(
        chosen, cpool[...], (((0,), (0,)), ((), ())), preferred_element_type=F32
    ).astype(BF16)

    def select_chunk(k, _):
        row = jnp.broadcast_to(rows_ref[pl.ds(k, 1), :].astype(F32), (128, 128))
        col = jnp.concatenate([row.T.astype(jnp.int32)] * (npool // 128), axis=1)
        hit = col == lax.broadcasted_iota(jnp.int32, (128, npool), 1)
        sel[pl.ds(pl.multiple_of(k * 128, 128), 128), :] = hit.astype(F32).astype(BF16)
        return 0

    lax.fori_loop(0, npts // 128, select_chunk, 0)
    get_coefs.wait()
    pl.semaphore_wait(barrier, len(dests))

    def spread_first():
        block = cen.at[0, 0, 0]
        for i in (1, 2):
            send(block, cen.at[0, 0, NEG[i]], send1.at[i], recv_p.at[0, NEG[i]], f=OFFS[i])
        send(block.at[0:half], cen.at[0, 0, 3, 0:half], send1.at[0], recv_p.at[0, 3], f=2)
        send(block.at[half:ncen], cen.at[0, 0, 3, half:ncen], send1.at[3], recv_p.at[0, 3], f=-2)

    def spread_second(i):
        block = cen.at[0, 0, i]
        for j in (1, 2):
            send(block, cen.at[NEG[j], 0, i], send2.at[i, j], recv_p.at[NEG[j], i], s=OFFS[j])
        send(block.at[0:half], cen.at[3, 0, i, 0:half], send2.at[i, 0], recv_p.at[3, i], s=2)
        send(block.at[half:ncen], cen.at[3, 0, i, half:ncen], send2.at[i, 3], recv_p.at[3, i], s=-2)

    def share(j, i):
        send(cen.at[j, 0, i], cen.at[j, 1, i], send_c.at[j, i], recv_q.at[j, i], partner=True)

    spread_first()
    spread_second(0)
    share(0, 0)

    get_pool.wait()

    def gather_chunk(n, _):
        cols = pl.ds(pl.multiple_of(n * 256, 256), 256)
        got = jnp.dot(sel[...], pool[:, cols], preferred_element_type=F32)
        pts[:, cols] = got.astype(BF16)
        square = jnp.sum(got * got, axis=1, keepdims=True)

        @pl.when(n == 0)
        def _():
            pnorm[...] = square

        @pl.when(n > 0)
        def _():
            pnorm[...] += square

        return 0

    lax.fori_loop(0, d // 256, gather_chunk, 0)

    for i in (1, 2, 3):
        arrived(cen.at[0, 0, i], recv_p.at[0, i])
        spread_second(i)
        share(0, i)

    get_targ.wait()

    def group_work(j):
        centers = cen[j, :, :, :, 0:d].reshape(group, d)
        weights = cen[j, :, :, :, d : d + outs].reshape(group, outs)
        square = centers.astype(F32)
        square = square * square
        part = square[:, 0:128]
        for t in range(1, d // 128):
            part = part + square[:, t * 128 : (t + 1) * 128]
        cnorm = jnp.sum(part.T, axis=0, keepdims=True)
        step = npts // 4

        def rows_work(r, _):
            rows = pl.ds(pl.multiple_of(r * step, step), step)
            inner = lax.dot_general(
                pts[rows, :], centers, (((1,), (1,)), ((), ())), preferred_element_type=F32
            )
            distance = pnorm[rows, :] + cnorm - 2.0 * inner
            block = jnp.exp(distance * (-1.0 / d)).astype(BF16)
            kern[rows, j * group : (j + 1) * group] = block
            term = jnp.dot(block, weights, preferred_element_type=F32)
            if j == 0:
                pred[rows, :] = term - targ[rows, :].astype(F32)
            else:
                pred[rows, :] += term
            return 0

        lax.fori_loop(0, 4, rows_work, 0)

    for j in range(4):
        if j:
            for i in range(4):
                arrived(cen.at[j, 0, i], recv_p.at[j, i])
                share(j, i)
        for i in range(4):
            arrived(cen.at[j, 1, i], recv_q.at[j, i])
        group_work(j)

    put_res = pltpu.make_async_copy(pred, res_hbm, lsem.at[0])
    put_res.start()
    resb[...] = pred[...].astype(BF16)

    def grad_of(j, parity):
        first = j * group + parity * (group // 2)
        return lax.dot_general(
            kern[:, first : first + group // 2], resb[...], (((0,), (0,)), ((), ())),
            preferred_element_type=F32,
        )

    quarter = group // 4
    order = (3, 1, 2, 0)
    for j in order:
        gq[j] = grad_of(j, 1)
        send(gq.at[j], gq_in.at[j], sgq.at[j], rgq.at[j], partner=True)
    for j in order:
        mine = grad_of(j, 0)
        arrived(gq_in.at[j], rgq.at[j])
        both = mine + gq_in[j]
        if j:
            gs[j] = both.astype(BF16)
            if j == 3:
                send(gs.at[3, 0:quarter], gs_in.at[3, 0:quarter], sgs.at[3], rgs.at[3], s=2)
                send(gs.at[3, quarter : 2 * quarter], gs_in.at[3, quarter : 2 * quarter], sgs.at[0], rgs.at[3], s=-2)
            else:
                send(gs.at[j], gs_in.at[NEG[j]], sgs.at[j], rgs.at[NEG[j]], s=OFFS[j])
        else:
            total = both
    for j in (1, 2, 3):
        arrived(gs_in.at[j], rgs.at[j])
        total = total + gs_in[j].astype(F32)
    gf[...] = total.reshape(gf.shape)

    eighth = gf.shape[2]
    for i in range(4):
        for k in range(4):
            if i or k:
                df, dx = fx_offset(i, k)
                piece = (here[0] + dx + NX) % NX
                send(gf.at[i, piece], gf_in.at[NEG[i], NEG[k]], sgf.at[i, k], rgf.at[NEG[i], NEG[k]], f=df, x=dx)
    mine = gf[0, here[0]]
    for i in range(4):
        for k in range(4):
            if i or k:
                arrived(gf_in.at[i, k], rgf.at[i, k])
                mine = mine + gf_in[i, k]

    gz[...] = mine
    for k, dz in enumerate((4, -4, 8)):
        send(gz, gz_in.at[k], sgz.at[k], rgz.at[k], z=dz)
    for k in range(3):
        arrived(gz_in.at[k], rgz.at[k])
    out[here[0]] = (mine + gz_in[0]) + (gz_in[1] + gz_in[2])
    for k in (1, 2, 3):
        send(out.at[here[0]], out.at[here[0]], sgx.at[k], rgx.at[NEG[k]], x=OFFS[k])
    for k in (1, 2, 3):
        arrived(out.at[(here[0] + OFFS[k] + NX) % NX], rgx.at[k])
    grad_ref[...] = out[...].reshape(grad_ref.shape)

    for copy in pending:
        copy.wait_send()
    put_res.wait()


def per_device(point_pool, batch_rows, targets, center_pool, center_rows, coefs):
    npool, d = point_pool.shape
    npts, outs = targets.shape
    ncen = coefs.shape[0]
    vmem = pl.BlockSpec(memory_space=pltpu.VMEM)
    anys = pl.BlockSpec(memory_space=pl.ANY)
    dma = pltpu.SemaphoreType.DMA
    half = 4 * ncen
    sub = ncen // NX
    scratch = [
        pltpu.VMEM((4, 2, 4, ncen, d + outs), BF16),
        pltpu.VMEM((npool, d), BF16),
        pltpu.VMEM((npts, npool), BF16),
        pltpu.VMEM((npts, d), BF16),
        pltpu.VMEM((npts, 1), F32),
        pltpu.VMEM((npts, 32 * ncen), BF16),
        pltpu.VMEM((npts, outs), F32),
        pltpu.VMEM((npts, outs), BF16),
        pltpu.VMEM((npts, outs), BF16),
        pltpu.VMEM(center_pool.shape, BF16),
        pltpu.VMEM((4, half, outs), F32),
        pltpu.VMEM((4, half, outs), F32),
        pltpu.VMEM((4, half, outs), BF16),
        pltpu.VMEM((4, half, outs), BF16),
        pltpu.VMEM((4, NX, sub, outs), F32),
        pltpu.VMEM((4, NX, sub, outs), F32),
        pltpu.VMEM((sub, outs), F32),
        pltpu.VMEM((3, sub, outs), F32),
        pltpu.VMEM((NX, sub, outs), F32),
        dma((4,)), dma((4,)), dma((4, 4)), dma((4, 4)), dma((4, 4)), dma((4, 4)),
        dma((4,)), dma((4,)), dma((4,)), dma((4,)), dma((4, 4)), dma((4, 4)),
        dma((3,)), dma((3,)), dma((4,)), dma((4,)),
    ]
    return pl.pallas_call(
        kernel,
        out_shape=(
            jax.ShapeDtypeStruct((npts, outs), F32),
            jax.ShapeDtypeStruct((ncen, outs), F32),
        ),
        in_specs=[anys, vmem, anys, anys, vmem, anys],
        out_specs=(anys, vmem),
        scratch_shapes=scratch,
        compiler_params=pltpu.CompilerParams(
            collective_id=0, has_side_effects=True, vmem_limit_bytes=56 << 20
        ),
        name="regression",
    )(
        point_pool, batch_rows.reshape(-1, 128), targets, center_pool,
        center_rows.reshape(1, -1), coefs,
    )


def solution(mesh):
    both = ("blk", "rep")
    in_specs = (P(both, None), P(both), P(both, None), P("blk", None), P("blk"), P("blk", None))
    out_specs = (P(both, None), P("blk", None))
    return jax.shard_map(per_device, mesh=mesh, in_specs=in_specs, out_specs=out_specs, check_vma=False)
```

time: 143 us -> 67 us (0.47)
  the two profiles are of different devices: /device:TPU:9 before, /device:TPU:2 now
where the time goes in v1:
time: 67 us; the launch traced here: 66.8 us
  Pallas kernels  62.5 us (93%)
  local copies, waits for them, and re-layouts  3.64 us (5%)
    pallas_call x1, Pallas kernels, per_device(): pl.pallas_call(kernel, out_shape=(jax.ShapeDtypeStruct((npts, outs), F32)...  62.5 us
    unnamed x2, local copies, waits for them, and re-layouts  3.64 us

profile of v1, /device:TPU:2, one launch (start us, length us, event | category | flops | bytes accessed | tf_op | source)
XLA Modules:
  0.0 66.8 jit_solution(2335775302748119069)
XLA Ops:
  0.6 62.5 %regression.1 = (f32[1024,256]{1,0:T(8,128)}, f32[32,256]{1,0:T(8,128)}) custom-call(bf16[1280,1024]{1,0:T(8,128)(2,1)} %pool_hbm.1, s32[8,128]{1,0:T(8,128)} %bitcast.2, bf16[1024,256]{1,0:T(8,128)(2,1)} %targets_hbm.1, bf16[64,1024]{1,0:T(8,128)(2,1)} %cpool_hbm.1, s32[1,32]{1,0:T(1,128)} %bitcast.3, bf16[32,256]{1,0:T(8,128)(2,1)} %coefs_hbm.1), custom_call_target="tpu_custom_call" | custom-call | tf_op jit(solution)/shard_map/regression/pallas_call | solution.py:308
  63.1 2.3 %copy.10 = f32[1024,256]{1,0:T(8,128)} copy(f32[1024,256]{1,0:T(8,128)} %get-tuple-element.4) | data formatting | bytes 2097152
  65.4 1.4 %copy.11 = f32[32,256]{1,0:T(8,128)} copy(f32[32,256]{1,0:T(8,128)} %get-tuple-element.5) | data formatting | bytes 65536

commit v2 on v1

v2 whole, which is shorter than its diff:
```python
import functools

import jax
import jax.numpy as jnp
from jax import lax
from jax.experimental import pallas as pl
from jax.experimental.pallas import tpu as pltpu
from jax.sharding import PartitionSpec as P

MESH = pl.DeviceIdType.MESH
F32 = jnp.float32
BF16 = jnp.bfloat16
OFFS = (0, 1, -1, 2)
NEG = (0, 2, 1, 3)
NX, NY, NL, NH, NZ = 4, 4, 4, 4, 16
STEPS = 1
S_STAGE = True
SF = ()
KT = True


def place():
    b = lax.axis_index("blk")
    r = lax.axis_index("rep")
    core = lax.rem(b, 2)
    z = lax.rem(r, NH) * NL + lax.rem(lax.div(b, 2), NL)
    return (lax.div(r, NH), lax.div(b, 2 * NL), z, core)


def at(here, f=0, s=0, x=0, z=0, partner=False):
    px, py, pz, core = here
    nx = lax.rem(px + (x + NX), NX)
    ny = lax.rem(py + (1 - core) * f + core * s + NY, NY)
    nz = lax.rem(pz + core * f + (1 - core) * s + (z + NZ), NZ)
    nc = 1 - core if partner else core
    return {"blk": (ny * NL + lax.rem(nz, NL)) * 2 + nc, "rep": nx * NH + lax.div(nz, NL)}


def fx_offset(i, j):
    df = OFFS[i]
    if df == 2 and j in (1, 2):
        df = -2
    return df, OFFS[j]


def destinations():
    out = [dict(partner=True)]
    for k in (1, -1, 2, -2):
        out += [dict(f=k), dict(s=k)]
    for k in (1, -1, 2):
        out.append(dict(x=k))
    return out


def opposite(offset):
    return {k: (v if k == "partner" else -v) for k, v in offset.items()}


def kernel(
    pool_hbm, rows_ref, targ, cpool, crows_ref, coefs_ref,
    res, grad_ref,
    cen, pool, sel, pts, pnorm, kern, resb,
    gq, gq_in, gs, gs_in, gf, gf_in, gz, gz_in, out,
    lsem, send1, send2, send_c, recv_p, recv_q,
    sgq, rgq, sgs, rgs, sgf, rgf, sgz, rgz, sgx, rgx, relay,
):
    npts, d = pts.shape
    npool = pool.shape[0]
    ncen, outs = coefs_ref.shape
    group = 8 * ncen
    half = ncen // 2

    get_pool = pltpu.make_async_copy(pool_hbm, pool, lsem.at[0])
    get_pool.start()

    here = place()
    known = {}

    def device(**offset):
        key = tuple(sorted(offset.items()))
        if key not in known:
            known[key] = at(here, **offset)
        return known[key]

    barrier = pltpu.get_barrier_semaphore()
    dests = destinations()
    for offset in dests:
        pl.semaphore_signal(barrier, inc=1, device_id=device(**opposite(offset)), device_id_type=MESH)

    pending = []

    def send(src, dst, ssem, rsem, **offset):
        copy = pltpu.make_async_remote_copy(
            src_ref=src, dst_ref=dst, send_sem=ssem, recv_sem=rsem,
            device_id=device(**offset), device_id_type=MESH,
        )
        copy.start()
        pending.append(copy)


    def arrived(ref, rsem):
        pltpu.make_async_remote_copy(
            src_ref=ref, dst_ref=ref, send_sem=sgx.at[0], recv_sem=rsem,
            device_id=device(partner=True), device_id_type=MESH,
        ).wait_recv()

    chosen = (
        lax.broadcasted_iota(jnp.int32, (cpool.shape[0], ncen), 0) == crows_ref[...]
    ).astype(F32).astype(BF16)
    cen[0, 0, :, 0:d] = lax.dot_general(
        chosen, cpool[...], (((0,), (0,)), ((), ())), preferred_element_type=F32
    ).astype(BF16)
    cen[0, 0, :, d : d + outs] = coefs_ref[...]

    def select_chunk(k, _):
        row = jnp.broadcast_to(rows_ref[pl.ds(k, 1), :].astype(F32), (128, 128))
        col = jnp.concatenate([row.T.astype(jnp.int32)] * (npool // 128), axis=1)
        hit = col == lax.broadcasted_iota(jnp.int32, (128, npool), 1)
        sel[pl.ds(pl.multiple_of(k * 128, 128), 128), :] = hit.astype(F32).astype(BF16)
        return 0

    pl.semaphore_wait(barrier, len(dests))

    def signal_relay(k, **offset):
        pl.semaphore_signal(relay.at[k], inc=1, device_id=device(**offset), device_id_type=MESH)

    own = (0, 2, 3, 6)
    other = (1, 4, 5, 7)

    def spread_first():
        block = cen.at[0, 0]
        send(block.at[0:half], cen.at[own[3], 0, 0:half], send1.at[0], recv_p.at[3, 0], f=2)
        send(block.at[half:ncen], cen.at[own[3], 0, half:ncen], send1.at[3], recv_p.at[3, 0], f=-2)
        for i in (1, 2):
            send(block, cen.at[own[NEG[i]], 0], send1.at[i], recv_p.at[NEG[i], 0], f=OFFS[i])

    def spread_second(i):
        block = cen.at[own[i], 0]
        if i not in SF:
            send(block.at[0:half], cen.at[own[i], 3, 0:half], send2.at[i, 0], recv_p.at[i, 3], s=2)
            send(block.at[half:ncen], cen.at[own[i], 3, half:ncen], send2.at[i, 3], recv_p.at[i, 3], s=-2)
        for j in (1, 2):
            send(block, cen.at[own[i], NEG[j]], send2.at[i, j], recv_p.at[i, NEG[j]], s=OFFS[j])

    def take(i, j):
        if i or j:
            arrived(cen.at[own[i], j], recv_p.at[i, j])
        if i in SF and j == 1:
            rows = slice(0, half)
            send(cen.at[own[i], 1, rows], cen.at[own[i], 3, rows], send2.at[i, 0], recv_p.at[i, 3], s=-1)
        if i in SF and j == 2:
            rows = slice(half, ncen)
            send(cen.at[own[i], 2, rows], cen.at[own[i], 3, rows], send2.at[i, 3], recv_p.at[i, 3], s=1)
        send(cen.at[own[i], j], cen.at[other[i], j], send_c.at[i, j], recv_q.at[i, j], partner=True)

    def take_other(i):
        for j in range(4):
            arrived(cen.at[other[i], j], recv_q.at[i, j])

    def gather_chunk(n):
        cols = slice(n * 256, n * 256 + 256)
        got = jnp.dot(sel[...], pool[:, cols], preferred_element_type=F32)
        pts[:, cols] = got.astype(BF16)
        square = jnp.sum(got * got, axis=1, keepdims=True)
        if n == 0:
            pnorm[...] = square
        else:
            pnorm[...] += square

    def group_work(g):
        centers = cen[2 * g : 2 * g + 2, :, :, 0:d].reshape(group, d)
        weights = cen[2 * g : 2 * g + 2, :, :, d : d + outs].reshape(group, outs)
        square = centers.astype(F32)
        square = square * square
        part = square[:, 0:128]
        for t in range(1, d // 128):
            part = part + square[:, t * 128 : (t + 1) * 128]
        cnorm = jnp.sum(part.T, axis=0, keepdims=True)
        step = npts // STEPS

        def rows_work(r, _):
            rows = pl.ds(pl.multiple_of(r * step, step), step)
            inner = lax.dot_general(
                pts[rows, :], centers, (((1,), (1,)), ((), ())), preferred_element_type=F32
            )
            distance = pnorm[rows, :] + cnorm - 2.0 * inner
            block = jnp.exp(distance * (-1.0 / d)).astype(BF16)
            if KT:
                kern[g * group : (g + 1) * group, rows] = block.T
            else:
                kern[rows, g * group : (g + 1) * group] = block
            term = jnp.dot(block, weights, preferred_element_type=F32)
            if g == 0:
                res[rows, :] = term - targ[rows, :].astype(F32)
            elif g < 3:
                res[rows, :] += term
            else:
                last = res[rows, :] + term
                res[rows, :] = last
                resb[rows, :] = last.astype(BF16)
            return 0

        lax.fori_loop(0, STEPS, rows_work, 0)

    spread_first()
    take(0, 0)
    for k in (1, -1, 2, -2):
        signal_relay(0, f=k)
    for k in (2, -2):
        signal_relay(0, s=k)
    lax.fori_loop(0, npts // 128, select_chunk, 0)
    spread_second(0)
    get_pool.wait()
    gather_chunk(0)
    gather_chunk(1)
    take(1, 0)
    spread_second(1)
    take(2, 0)
    spread_second(2)
    gather_chunk(2)
    take(3, 0)
    spread_second(3)
    take(0, 1)
    take(0, 2)
    gather_chunk(3)
    pl.semaphore_wait(relay.at[0], 6)
    signal_relay(1, z=4)
    signal_relay(1, z=-4)
    take(0, 3)
    take(1, 1)
    take(1, 2)
    take_other(0)
    group_work(0)
    take(2, 1)
    take(2, 2)
    take(3, 1)
    take(3, 2)
    take(1, 3)
    take(2, 3)
    group_work(1)
    take(3, 3)
    take_other(1)
    take_other(2)
    group_work(2)
    take_other(3)
    group_work(3)
    pl.semaphore_wait(relay.at[1], 2)

    def grad_of(slot):
        part = slice(slot * 4 * ncen, (slot + 1) * 4 * ncen)
        if KT:
            return jnp.dot(kern[part, :], resb[...], preferred_element_type=F32)
        return lax.dot_general(
            kern[:, part], resb[...], (((0,), (0,)), ((), ())), preferred_element_type=F32
        )

    for i in range(4):
        gq[i] = grad_of(other[i])
        send(gq.at[i], gq_in.at[i], sgq.at[i], rgq.at[i], partner=True)
    total = []
    for i in range(4):
        mine = grad_of(own[i])
        arrived(gq_in.at[i], rgq.at[i])
        both = mine + gq_in[i]
        total.append(both[0:ncen])
        for j in (1, 2, 3):
            gs[j, i] = both[j * ncen : (j + 1) * ncen].astype(BF16)
        if S_STAGE and i == 1:
            send(gs.at[3, 0:2], gs_in.at[3, 0:2], sgs.at[3], rgs.at[3], s=2)
        if S_STAGE and i == 3:
            send(gs.at[3, 2:4], gs_in.at[3, 2:4], sgs.at[0], rgs.at[3], s=-2)
            for j in (1, 2):
                send(gs.at[j], gs_in.at[NEG[j]], sgs.at[j], rgs.at[NEG[j]], s=OFFS[j])
    for j in (1, 2, 3):
        arrived(gs_in.at[j], rgs.at[j])
    eighth = ncen // NX
    for i in (3, 1, 2, 0):
        whole = total[i] + gs_in[1, i].astype(F32) + gs_in[2, i].astype(F32) + gs_in[3, i].astype(F32)
        gf[i] = whole.reshape(NX, eighth, outs)
    for i in (3, 1, 2, 0):
        for k in (3, 1, 2, 0):
            if i or k:
                df, dx = fx_offset(i, k)
                piece = lax.rem(here[0] + (dx + NX), NX)
                send(gf.at[i, piece], gf_in.at[NEG[i], NEG[k]], sgf.at[i, k], rgf.at[NEG[i], NEG[k]], f=df, x=dx)
    mine = gf[0, here[0]]
    for i in range(4):
        for k in range(4):
            if i or k:
                arrived(gf_in.at[i, k], rgf.at[i, k])
                mine = mine + gf_in[i, k]

    gz[...] = mine
    for k, dz in enumerate((4, -4, 8)):
        send(gz, gz_in.at[k], sgz.at[k], rgz.at[k], z=dz)
    for k in range(3):
        arrived(gz_in.at[k], rgz.at[k])
    out[here[0]] = (mine + gz_in[0]) + (gz_in[1] + gz_in[2])
    for k in (3, 1, 2):
        send(out.at[here[0]], out.at[here[0]], sgx.at[k], rgx.at[NEG[k]], x=OFFS[k])
    for k in (1, 2, 3):
        arrived(out.at[lax.rem(here[0] + (OFFS[k] + NX), NX)], rgx.at[k])
    grad_ref[...] = out[...].reshape(grad_ref.shape)

    for copy in pending:
        copy.wait_send()


def per_device(point_pool, batch_rows, targets, center_pool, center_rows, coefs):
    npool, d = point_pool.shape
    npts, outs = targets.shape
    ncen = coefs.shape[0]
    vmem = pl.BlockSpec(memory_space=pltpu.VMEM)
    anys = pl.BlockSpec(memory_space=pl.ANY)
    dma = pltpu.SemaphoreType.DMA
    half = 4 * ncen
    sub = ncen // NX
    scratch = [
        pltpu.VMEM((8, 4, ncen, d + outs), BF16),
        pltpu.VMEM((npool, d), BF16),
        pltpu.VMEM((npts, npool), BF16),
        pltpu.VMEM((npts, d), BF16),
        pltpu.VMEM((npts, 1), F32),
        pltpu.VMEM((npts, 32 * ncen), BF16),
        pltpu.VMEM((npts, outs), BF16),
        pltpu.VMEM((4, half, outs), F32),
        pltpu.VMEM((4, half, outs), F32),
        pltpu.VMEM((4, 4, ncen, outs), BF16),
        pltpu.VMEM((4, 4, ncen, outs), BF16),
        pltpu.VMEM((4, NX, sub, outs), F32),
        pltpu.VMEM((4, NX, sub, outs), F32),
        pltpu.VMEM((sub, outs), F32),
        pltpu.VMEM((3, sub, outs), F32),
        pltpu.VMEM((NX, sub, outs), F32),
        dma((1,)), dma((4,)), dma((4, 4)), dma((4, 4)), dma((4, 4)), dma((4, 4)),
        dma((4,)), dma((4,)), dma((4,)), dma((4,)), dma((4, 4)), dma((4, 4)),
        dma((3,)), dma((3,)), dma((4,)), dma((4,)), pltpu.SemaphoreType.REGULAR((2,)),
    ]
    return pl.pallas_call(
        kernel,
        out_shape=(
            jax.ShapeDtypeStruct((npts, outs), F32),
            jax.ShapeDtypeStruct((ncen, outs), F32),
        ),
        in_specs=[anys, vmem, vmem, vmem, vmem, vmem],
        out_specs=(vmem, vmem),
        scratch_shapes=scratch,
        compiler_params=pltpu.CompilerParams(
            collective_id=0, has_side_effects=True, vmem_limit_bytes=52 << 20
        ),
        name="regression",
    )(
        point_pool, batch_rows.reshape(-1, 128), targets, center_pool,
        center_rows.reshape(1, -1), coefs,
    )


def solution(mesh):
    both = ("blk", "rep")
    in_specs = (P(both, None), P(both), P(both, None), P("blk", None), P("blk"), P("blk", None))
    out_specs = (P(both, None), P("blk", None))
    return jax.shard_map(per_device, mesh=mesh, in_specs=in_specs, out_specs=out_specs, check_vma=False)
```

time: 67 us -> 61.4 us (0.916)
  Pallas kernels: 62.5 us -> 54.9 us
  local copies, waits for them, and re-layouts: 3.64 us -> 5.58 us
    pallas_call x1, Pallas kernels: 62.5 us -> 54.9 us  [per_device(): pl.pallas_call(kernel, out_shape=(jax.ShapeDtypeStruct((npts, outs), F32)...]
    unnamed x2 -> x12, local copies, waits for them, and re-layouts: 3.64 us -> 5.58 us
where the time goes in v2:
time: 61.4 us; the launch traced here: 61.1 us
  Pallas kernels  54.9 us (89%)
  local copies, waits for them, and re-layouts  5.58 us (9%)
  between operations  0.65 us (1%)
    pallas_call x1, Pallas kernels, per_device(): pl.pallas_call(kernel, out_shape=(jax.ShapeDtypeStruct((npts, outs), F32)...  54.9 us
    unnamed x12, local copies, waits for them, and re-layouts  5.58 us

profile of v2, /device:TPU:2, one launch (start us, length us, event | category | flops | bytes accessed | tf_op | source)
XLA Modules:
  0.0 61.1 jit_solution(14315789836540114958)
XLA Ops:
  0.6 0.0 copy-start
  0.6 1.0 %copy-done = bf16[1024,256]{1,0:T(8,128)(2,1)S(1)} copy-done((bf16[1024,256]{1,0:T(8,128)(2,1)S(1)}, bf16[1024,256]{1,0:T(8,128)(2,1)}, u32[]{:S(2)}) %copy-start) | copy-done | bytes 524312
  1.7 0.0 copy-start.1
  1.7 0.9 %copy-done.1 = bf16[64,1024]{1,0:T(8,128)(2,1)S(1)} copy-done((bf16[64,1024]{1,0:T(8,128)(2,1)S(1)}, bf16[64,1024]{1,0:T(8,128)(2,1)}, u32[]{:S(2)}) %copy-start.1) | copy-done | bytes 131096
  2.6 0.0 copy-start.2
  2.6 0.7 %copy-done.2 = bf16[32,256]{1,0:T(8,128)(2,1)S(1)} copy-done((bf16[32,256]{1,0:T(8,128)(2,1)S(1)}, bf16[32,256]{1,0:T(8,128)(2,1)}, u32[]{:S(2)}) %copy-start.2) | copy-done | bytes 16408
  3.3 0.0 copy-start.3
  3.3 0.7 %copy-done.3 = s32[1024]{0:T(1024)S(1)} copy-done((s32[1024]{0:T(1024)S(1)}, s32[1024]{0:T(1024)}, u32[]{:S(2)}) %copy-start.3) | copy-done | bytes 4120
  4.0 0.0 copy-start.4
  4.0 0.7 %copy-done.4 = s32[32]{0:T(128)S(1)} copy-done((s32[32]{0:T(128)S(1)}, s32[32]{0:T(128)}, u32[]{:S(2)}) %copy-start.4) | copy-done | bytes 152
  4.6 54.9 %regression.1 = (f32[1024,256]{1,0:T(8,128)S(1)}, f32[32,256]{1,0:T(8,128)S(1)}) custom-call(bf16[1280,1024]{1,0:T(8,128)(2,1)} %pool_hbm.1, s32[8,128]{1,0:T(8,128)S(1)} %bitcast.2, bf16[1024,256]{1,0:T(8,128)(2,1)S(1)} %copy-done, bf16[64,1024]{1,0:T(8,128)(2,1)S(1)} %copy-done.1, s32[1,32]{1,0:T(1,128)S(1)} %bitcast.3, bf16[32,256]{1,0:T(8,128)(2,1)S(1)} %copy-done.2), custom_call_target="tpu_custom_call" | custom-call | tf_op jit(solution)/shard_map/regression/pallas_call | solution.py:339
  59.5 1.0 %copy.10 = f32[1024,256]{1,0:T(8,128)} copy(f32[1024,256]{1,0:T(8,128)S(1)} %get-tuple-element.4) | data formatting | bytes 2097152
  60.5 0.6 %copy.11 = f32[32,256]{1,0:T(8,128)} copy(f32[32,256]{1,0:T(8,128)S(1)} %get-tuple-element.5) | data formatting | bytes 65536
Async XLA Ops:
  0.6 1.0 %copy-start = (bf16[1024,256]{1,0:T(8,128)(2,1)S(1)}, bf16[1024,256]{1,0:T(8,128)(2,1)}, u32[]{:S(2)}) copy-start(bf16[1024,256]{1,0:T(8,128)(2,1)} %targ.1) | copy-start | bytes 1572868
  1.7 0.9 %copy-start.1 = (bf16[64,1024]{1,0:T(8,128)(2,1)S(1)}, bf16[64,1024]{1,0:T(8,128)(2,1)}, u32[]{:S(2)}) copy-start(bf16[64,1024]{1,0:T(8,128)(2,1)} %cpool.1) | copy-start | bytes 393220
  2.6 0.7 %copy-start.2 = (bf16[32,256]{1,0:T(8,128)(2,1)S(1)}, bf16[32,256]{1,0:T(8,128)(2,1)}, u32[]{:S(2)}) copy-start(bf16[32,256]{1,0:T(8,128)(2,1)} %coefs_ref.1) | copy-start | bytes 49156
  3.3 0.7 %copy-start.3 = (s32[1024]{0:T(1024)S(1)}, s32[1024]{0:T(1024)}, u32[]{:S(2)}) copy-start(s32[1024]{0:T(1024)} %param.7) | copy-start | bytes 12292
  4.0 0.7 %copy-start.4 = (s32[32]{0:T(128)S(1)}, s32[32]{0:T(128)}, u32[]{:S(2)}) copy-start(s32[32]{0:T(128)} %param.10) | copy-start | bytes 388

commit v3 on v2

--- a/solution.py
+++ b/solution.py
@@ -14,9 +14,22 @@
 NEG = (0, 2, 1, 3)
 NX, NY, NL, NH, NZ = 4, 4, 4, 4, 16
 STEPS = 1
-S_STAGE = True
-SF = ()
-KT = True
+PLAN = (
+    ("first",), ("take", 0, 0), ("near",), ("select",), ("second", 0),
+    ("gather", 0), ("gather", 1),
+    ("take", 1, 0), ("second", 1), ("take", 2, 0), ("second", 2),
+    ("gather", 2),
+    ("take", 3, 0), ("second", 3), ("take", 0, 1), ("take", 0, 2),
+    ("gather", 3), ("far",),
+    ("take", 0, 3), ("take", 1, 1), ("take", 1, 2), ("other", 0),
+    ("group", 0),
+    ("take", 2, 1), ("take", 2, 2), ("take", 3, 1), ("take", 3, 2), ("take", 1, 3), ("take", 2, 3),
+    ("group", 1),
+    ("take", 3, 3), ("other", 1), ("other", 2),
+    ("group", 2),
+    ("other", 3),
+    ("group", 3),
+)
 
 
 def place():
@@ -57,21 +70,27 @@
 
 
 def kernel(
-    pool_hbm, rows_ref, targ, cpool, crows_ref, coefs_ref,
+    pool_hbm, rows_hbm, targ_hbm, cpool_hbm, crows_hbm, coefs_hbm,
     res, grad_ref,
-    cen, pool, sel, pts, pnorm, kern, resb,
+    cen, pool, sel, pts, pnorm, kern, resb, targ, cpool, rows_ref, crows_ref,
     gq, gq_in, gs, gs_in, gf, gf_in, gz, gz_in, out,
     lsem, send1, send2, send_c, recv_p, recv_q,
     sgq, rgq, sgs, rgs, sgf, rgf, sgz, rgz, sgx, rgx, relay,
 ):
     npts, d = pts.shape
     npool = pool.shape[0]
-    ncen, outs = coefs_ref.shape
+    ncen, outs = coefs_hbm.shape
     group = 8 * ncen
     half = ncen // 2
 
+    get_crows = pltpu.make_async_copy(crows_hbm, crows_ref, lsem.at[1])
+    get_cpool = pltpu.make_async_copy(cpool_hbm, cpool, lsem.at[2])
+    get_coefs = pltpu.make_async_copy(coefs_hbm, cen.at[0, 0, :, pl.ds(d, outs)], lsem.at[3])
+    get_rows = pltpu.make_async_copy(rows_hbm, rows_ref, lsem.at[4])
     get_pool = pltpu.make_async_copy(pool_hbm, pool, lsem.at[0])
-    get_pool.start()
+    get_targ = pltpu.make_async_copy(targ_hbm, targ, lsem.at[5])
+    for copy in (get_crows, get_cpool, get_coefs, get_rows, get_pool, get_targ):
+        copy.start()
 
     here = place()
     known = {}
@@ -104,13 +123,17 @@
             device_id=device(partner=True), device_id_type=MESH,
         ).wait_recv()
 
+    get_crows.wait()
+    get_cpool.wait()
     chosen = (
         lax.broadcasted_iota(jnp.int32, (cpool.shape[0], ncen), 0) == crows_ref[...]
     ).astype(F32).astype(BF16)
     cen[0, 0, :, 0:d] = lax.dot_general(
         chosen, cpool[...], (((0,), (0,)), ((), ())), preferred_element_type=F32
     ).astype(BF16)
-    cen[0, 0, :, d : d + outs] = coefs_ref[...]
+    get_coefs.wait()
+    get_rows.wait()
+    get_targ.wait()
 
     def select_chunk(k, _):
         row = jnp.broadcast_to(rows_ref[pl.ds(k, 1), :].astype(F32), (128, 128))
@@ -136,21 +159,14 @@
 
     def spread_second(i):
         block = cen.at[own[i], 0]
-        if i not in SF:
-            send(block.at[0:half], cen.at[own[i], 3, 0:half], send2.at[i, 0], recv_p.at[i, 3], s=2)
-            send(block.at[half:ncen], cen.at[own[i], 3, half:ncen], send2.at[i, 3], recv_p.at[i, 3], s=-2)
+        send(block.at[0:half], cen.at[own[i], 3, 0:half], send2.at[i, 0], recv_p.at[i, 3], s=2)
+        send(block.at[half:ncen], cen.at[own[i], 3, half:ncen], send2.at[i, 3], recv_p.at[i, 3], s=-2)
         for j in (1, 2):
             send(block, cen.at[own[i], NEG[j]], send2.at[i, j], recv_p.at[i, NEG[j]], s=OFFS[j])
 
     def take(i, j):
         if i or j:
             arrived(cen.at[own[i], j], recv_p.at[i, j])
-        if i in SF and j == 1:
-            rows = slice(0, half)
-            send(cen.at[own[i], 1, rows], cen.at[own[i], 3, rows], send2.at[i, 0], recv_p.at[i, 3], s=-1)
-        if i in SF and j == 2:
-            rows = slice(half, ncen)
-            send(cen.at[own[i], 2, rows], cen.at[own[i], 3, rows], send2.at[i, 3], recv_p.at[i, 3], s=1)
         send(cen.at[own[i], j], cen.at[other[i], j], send_c.at[i, j], recv_q.at[i, j], partner=True)
 
     def take_other(i):
@@ -185,10 +201,7 @@
             )
             distance = pnorm[rows, :] + cnorm - 2.0 * inner
             block = jnp.exp(distance * (-1.0 / d)).astype(BF16)
-            if KT:
-                kern[g * group : (g + 1) * group, rows] = block.T
-            else:
-                kern[rows, g * group : (g + 1) * group] = block
+            kern[g * group : (g + 1) * group, rows] = block.T
             term = jnp.dot(block, weights, preferred_element_type=F32)
             if g == 0:
                 res[rows, :] = term - targ[rows, :].astype(F32)
@@ -202,57 +215,33 @@
 
         lax.fori_loop(0, STEPS, rows_work, 0)
 
-    spread_first()
-    take(0, 0)
-    for k in (1, -1, 2, -2):
-        signal_relay(0, f=k)
-    for k in (2, -2):
-        signal_relay(0, s=k)
-    lax.fori_loop(0, npts // 128, select_chunk, 0)
-    spread_second(0)
-    get_pool.wait()
-    gather_chunk(0)
-    gather_chunk(1)
-    take(1, 0)
-    spread_second(1)
-    take(2, 0)
-    spread_second(2)
-    gather_chunk(2)
-    take(3, 0)
-    spread_second(3)
-    take(0, 1)
-    take(0, 2)
-    gather_chunk(3)
-    pl.semaphore_wait(relay.at[0], 6)
-    signal_relay(1, z=4)
-    signal_relay(1, z=-4)
-    take(0, 3)
-    take(1, 1)
-    take(1, 2)
-    take_other(0)
-    group_work(0)
-    take(2, 1)
-    take(2, 2)
-    take(3, 1)
-    take(3, 2)
-    take(1, 3)
-    take(2, 3)
-    group_work(1)
-    take(3, 3)
-    take_other(1)
-    take_other(2)
-    group_work(2)
-    take_other(3)
-    group_work(3)
+    def relay_near():
+        for k in (1, -1, 2, -2):
+            signal_relay(0, f=k)
+        for k in (2, -2):
+            signal_relay(0, s=k)
+
+    def relay_far():
+        pl.semaphore_wait(relay.at[0], 6)
+        signal_relay(1, z=4)
+        signal_relay(1, z=-4)
+
+    def select():
+        lax.fori_loop(0, npts // 128, select_chunk, 0)
+        get_pool.wait()
+
+    steps = {
+        "first": spread_first, "second": spread_second, "take": take, "other": take_other,
+        "select": select, "gather": gather_chunk, "group": group_work,
+        "near": relay_near, "far": relay_far,
+    }
+    for name, *where in PLAN:
+        steps[name](*where)
     pl.semaphore_wait(relay.at[1], 2)
 
     def grad_of(slot):
         part = slice(slot * 4 * ncen, (slot + 1) * 4 * ncen)
-        if KT:
-            return jnp.dot(kern[part, :], resb[...], preferred_element_type=F32)
-        return lax.dot_general(
-            kern[:, part], resb[...], (((0,), (0,)), ((), ())), preferred_element_type=F32
-        )
+        return jnp.dot(kern[part, :], resb[...], preferred_element_type=F32)
 
     for i in range(4):
         gq[i] = grad_of(other[i])
@@ -265,9 +254,9 @@
         total.append(both[0:ncen])
         for j in (1, 2, 3):
             gs[j, i] = both[j * ncen : (j + 1) * ncen].astype(BF16)
-        if S_STAGE and i == 1:
+        if i == 1:
             send(gs.at[3, 0:2], gs_in.at[3, 0:2], sgs.at[3], rgs.at[3], s=2)
-        if S_STAGE and i == 3:
+        if i == 3:
             send(gs.at[3, 2:4], gs_in.at[3, 2:4], sgs.at[0], rgs.at[3], s=-2)
             for j in (1, 2):
                 send(gs.at[j], gs_in.at[NEG[j]], sgs.at[j], rgs.at[NEG[j]], s=OFFS[j])
@@ -307,6 +296,7 @@
 
 
 def per_device(point_pool, batch_rows, targets, center_pool, center_rows, coefs):
+    batch_rows, center_rows = batch_rows.reshape(-1, 128), center_rows.reshape(1, -1)
     npool, d = point_pool.shape
     npts, outs = targets.shape
     ncen = coefs.shape[0]
@@ -323,6 +313,10 @@
         pltpu.VMEM((npts, 1), F32),
         pltpu.VMEM((npts, 32 * ncen), BF16),
         pltpu.VMEM((npts, outs), BF16),
+        pltpu.VMEM((npts, outs), BF16),
+        pltpu.VMEM(center_pool.shape, BF16),
+        pltpu.VMEM((npts // 128, 128), jnp.int32),
+        pltpu.VMEM((1, ncen), jnp.int32),
         pltpu.VMEM((4, half, outs), F32),
         pltpu.VMEM((4, half, outs), F32),
         pltpu.VMEM((4, 4, ncen, outs), BF16),
@@ -332,7 +326,7 @@
         pltpu.VMEM((sub, outs), F32),
         pltpu.VMEM((3, sub, outs), F32),
         pltpu.VMEM((NX, sub, outs), F32),
-        dma((1,)), dma((4,)), dma((4, 4)), dma((4, 4)), dma((4, 4)), dma((4, 4)),
+        dma((6,)), dma((4,)), dma((4, 4)), dma((4, 4)), dma((4, 4)), dma((4, 4)),
         dma((4,)), dma((4,)), dma((4,)), dma((4,)), dma((4, 4)), dma((4, 4)),
         dma((3,)), dma((3,)), dma((4,)), dma((4,)), pltpu.SemaphoreType.REGULAR((2,)),
     ]
@@ -342,17 +336,17 @@
             jax.ShapeDtypeStruct((npts, outs), F32),
             jax.ShapeDtypeStruct((ncen, outs), F32),
         ),
-        in_specs=[anys, vmem, vmem, vmem, vmem, vmem],
+        in_specs=[anys] * 6,
         out_specs=(vmem, vmem),
         scratch_shapes=scratch,
         compiler_params=pltpu.CompilerParams(
-            collective_id=0, has_side_effects=True, vmem_limit_bytes=52 << 20
+            collective_id=0, has_side_effects=True, vmem_limit_bytes=44 << 20
         ),
         name="regression",
-    )(
-        point_pool, batch_rows.reshape(-1, 128), targets, center_pool,
-        center_rows.reshape(1, -1), coefs,
-    )
+    )(*(
+        pltpu.with_memory_space_constraint(a, pltpu.HBM)
+        for a in (point_pool, batch_rows, targets, center_pool, center_rows, coefs)
+    ))
 
 
 def solution(mesh):

time: 61.4 us -> 57.3 us (0.933)
  local copies, waits for them, and re-layouts: 5.58 us -> 1.59 us
    unnamed x12 -> x2, local copies, waits for them, and re-layouts: 5.58 us -> 1.59 us
where the time goes in v3:
time: 57.3 us; the launch traced here: 57.1 us
  Pallas kernels  54.9 us (96%)
  local copies, waits for them, and re-layouts  1.59 us (3%)
  between operations  0.64 us (1%)
    pallas_call x1, Pallas kernels, per_device(): pl.pallas_call(kernel, out_shape=(jax.ShapeDtypeStruct((npts, outs), F32)...  54.9 us
    unnamed x2, local copies, waits for them, and re-layouts  1.59 us

profile of v3, /device:TPU:2, one launch (start us, length us, event | category | flops | bytes accessed | tf_op | source)
XLA Modules:
  0.0 57.1 jit_solution(6888342566249357446)
XLA Ops:
  0.6 54.9 %regression.1 = (f32[1024,256]{1,0:T(8,128)S(1)}, f32[32,256]{1,0:T(8,128)S(1)}) custom-call(bf16[1280,1024]{1,0:T(8,128)(2,1)} %pool_hbm.1, s32[8,128]{1,0:T(8,128)} %bitcast.2, bf16[1024,256]{1,0:T(8,128)(2,1)} %targ_hbm.1, bf16[64,1024]{1,0:T(8,128)(2,1)} %cpool_hbm.1, s32[1,32]{1,0:T(1,128)} %bitcast.3, bf16[32,256]{1,0:T(8,128)(2,1)} %coefs_hbm.1), custom_call_target="tpu_custom_call" | custom-call | tf_op jit(solution)/shard_map/regression/pallas_call | solution.py:333
  55.6 1.0 %copy.10 = f32[1024,256]{1,0:T(8,128)} copy(f32[1024,256]{1,0:T(8,128)S(1)} %get-tuple-element.4) | data formatting | bytes 2097152
  56.5 0.6 %copy.11 = f32[32,256]{1,0:T(8,128)} copy(f32[32,256]{1,0:T(8,128)S(1)} %get-tuple-element.5) | data formatting | bytes 65536

commit v4 on v3

--- a/solution.py
+++ b/solution.py
@@ -19,13 +19,12 @@
     ("gather", 0), ("gather", 1),
     ("take", 1, 0), ("second", 1), ("take", 2, 0), ("second", 2),
     ("gather", 2),
-    ("take", 3, 0), ("second", 3), ("take", 0, 1), ("take", 0, 2),
-    ("gather", 3), ("far",),
-    ("take", 0, 3), ("take", 1, 1), ("take", 1, 2), ("other", 0),
+    ("take", 3, 0), ("second", 3), ("take", 0, 1), ("take", 0, 2), ("take", 0, 3),
+    ("gather", 3), ("far",), ("other", 0),
     ("group", 0),
-    ("take", 2, 1), ("take", 2, 2), ("take", 3, 1), ("take", 3, 2), ("take", 1, 3), ("take", 2, 3),
+    ("take", 1, 1), ("take", 1, 2), ("take", 2, 1), ("take", 2, 2), ("take", 1, 3), ("take", 2, 3),
     ("group", 1),
-    ("take", 3, 3), ("other", 1), ("other", 2),
+    ("take", 3, 1), ("take", 3, 2), ("take", 3, 3), ("other", 1), ("other", 2),
     ("group", 2),
     ("other", 3),
     ("group", 3),
@@ -254,12 +253,11 @@
         total.append(both[0:ncen])
         for j in (1, 2, 3):
             gs[j, i] = both[j * ncen : (j + 1) * ncen].astype(BF16)
-        if i == 1:
-            send(gs.at[3, 0:2], gs_in.at[3, 0:2], sgs.at[3], rgs.at[3], s=2)
-        if i == 3:
-            send(gs.at[3, 2:4], gs_in.at[3, 2:4], sgs.at[0], rgs.at[3], s=-2)
+        if i in (1, 3):
+            part = slice(i - 1, i + 1)
+            send(gs.at[3, part], gs_in.at[3, part], sgs.at[3, i], rgs.at[3], s=2 if i == 1 else -2)
             for j in (1, 2):
-                send(gs.at[j], gs_in.at[NEG[j]], sgs.at[j], rgs.at[NEG[j]], s=OFFS[j])
+                send(gs.at[j, part], gs_in.at[NEG[j], part], sgs.at[j, i], rgs.at[NEG[j]], s=OFFS[j])
     for j in (1, 2, 3):
         arrived(gs_in.at[j], rgs.at[j])
     eighth = ncen // NX
@@ -327,7 +325,7 @@
         pltpu.VMEM((3, sub, outs), F32),
         pltpu.VMEM((NX, sub, outs), F32),
         dma((6,)), dma((4,)), dma((4, 4)), dma((4, 4)), dma((4, 4)), dma((4, 4)),
-        dma((4,)), dma((4,)), dma((4,)), dma((4,)), dma((4, 4)), dma((4, 4)),
+        dma((4,)), dma((4,)), dma((4, 4)), dma((4,)), dma((4, 4)), dma((4, 4)),
         dma((3,)), dma((3,)), dma((4,)), dma((4,)), pltpu.SemaphoreType.REGULAR((2,)),
     ]
     return pl.pallas_call(

time: 57.3 us -> 55.7 us (0.972)
  Pallas kernels: 54.9 us -> 53.3 us
    pallas_call x1, Pallas kernels: 54.9 us -> 53.3 us  [per_device(): pl.pallas_call(kernel, out_shape=(jax.ShapeDtypeStruct((npts, outs), F32)...]
where the time goes in v4:
time: 55.7 us; the launch traced here: 55.6 us
  Pallas kernels  53.3 us (96%)
  local copies, waits for them, and re-layouts  1.59 us (3%)
  between operations  0.64 us (1%)
    pallas_call x1, Pallas kernels, per_device(): pl.pallas_call(kernel, out_shape=(jax.ShapeDtypeStruct((npts, outs), F32)...  53.3 us
    unnamed x2, local copies, waits for them, and re-layouts  1.59 us

profile of v4, /device:TPU:2, one launch (start us, length us, event | category | flops | bytes accessed | tf_op | source)
XLA Modules:
  0.0 55.6 jit_solution(2613018358302357718)
XLA Ops:
  0.6 53.3 %regression.1 = (f32[1024,256]{1,0:T(8,128)S(1)}, f32[32,256]{1,0:T(8,128)S(1)}) custom-call(bf16[1280,1024]{1,0:T(8,128)(2,1)} %pool_hbm.1, s32[8,128]{1,0:T(8,128)} %bitcast.2, bf16[1024,256]{1,0:T(8,128)(2,1)} %targ_hbm.1, bf16[64,1024]{1,0:T(8,128)(2,1)} %cpool_hbm.1, s32[1,32]{1,0:T(1,128)} %bitcast.3, bf16[32,256]{1,0:T(8,128)(2,1)} %coefs_hbm.1), custom_call_target="tpu_custom_call" | custom-call | tf_op jit(solution)/shard_map/regression/pallas_call | solution.py:331
  54.0 1.0 %copy.10 = f32[1024,256]{1,0:T(8,128)} copy(f32[1024,256]{1,0:T(8,128)S(1)} %get-tuple-element.4) | data formatting | bytes 2097152
  54.9 0.6 %copy.11 = f32[32,256]{1,0:T(8,128)} copy(f32[32,256]{1,0:T(8,128)S(1)} %get-tuple-element.5) | data formatting | bytes 65536

commit v5 on v4

--- a/solution.py
+++ b/solution.py
@@ -20,7 +20,7 @@
     ("take", 1, 0), ("second", 1), ("take", 2, 0), ("second", 2),
     ("gather", 2),
     ("take", 3, 0), ("second", 3), ("take", 0, 1), ("take", 0, 2), ("take", 0, 3),
-    ("gather", 3), ("far",), ("other", 0),
+    ("gather", 3), ("far",), ("ready",), ("other", 0),
     ("group", 0),
     ("take", 1, 1), ("take", 1, 2), ("take", 2, 1), ("take", 2, 2), ("take", 1, 3), ("take", 2, 3),
     ("group", 1),
@@ -88,7 +88,7 @@
     get_rows = pltpu.make_async_copy(rows_hbm, rows_ref, lsem.at[4])
     get_pool = pltpu.make_async_copy(pool_hbm, pool, lsem.at[0])
     get_targ = pltpu.make_async_copy(targ_hbm, targ, lsem.at[5])
-    for copy in (get_crows, get_cpool, get_coefs, get_rows, get_pool, get_targ):
+    for copy in (get_crows, get_cpool, get_coefs):
         copy.start()
 
     here = place()
@@ -105,7 +105,15 @@
     for offset in dests:
         pl.semaphore_signal(barrier, inc=1, device_id=device(**opposite(offset)), device_id_type=MESH)
 
+    for copy in (get_rows, get_pool, get_targ):
+        copy.start()
+
     pending = []
+
+    def sent():
+        for copy in pending:
+            copy.wait_send()
+        pending.clear()
 
     def send(src, dst, ssem, rsem, **offset):
         copy = pltpu.make_async_remote_copy(
@@ -114,7 +122,6 @@
         )
         copy.start()
         pending.append(copy)
-
 
     def arrived(ref, rsem):
         pltpu.make_async_remote_copy(
@@ -131,8 +138,6 @@
         chosen, cpool[...], (((0,), (0,)), ((), ())), preferred_element_type=F32
     ).astype(BF16)
     get_coefs.wait()
-    get_rows.wait()
-    get_targ.wait()
 
     def select_chunk(k, _):
         row = jnp.broadcast_to(rows_ref[pl.ds(k, 1), :].astype(F32), (128, 128))
@@ -148,6 +153,7 @@
 
     own = (0, 2, 3, 6)
     other = (1, 4, 5, 7)
+    row_of = {slot: k * 4 * ncen for k, slot in enumerate(own + other)}
 
     def spread_first():
         block = cen.at[0, 0]
@@ -200,7 +206,10 @@
             )
             distance = pnorm[rows, :] + cnorm - 2.0 * inner
             block = jnp.exp(distance * (-1.0 / d)).astype(BF16)
-            kern[g * group : (g + 1) * group, rows] = block.T
+            flipped = block.T
+            for k in (2 * g, 2 * g + 1):
+                at_row = row_of[k]
+                kern[at_row : at_row + group // 2, rows] = flipped[(k % 2) * group // 2 : (k % 2 + 1) * group // 2]
             term = jnp.dot(block, weights, preferred_element_type=F32)
             if g == 0:
                 res[rows, :] = term - targ[rows, :].astype(F32)
@@ -226,6 +235,7 @@
         signal_relay(1, z=-4)
 
     def select():
+        get_rows.wait()
         lax.fori_loop(0, npts // 128, select_chunk, 0)
         get_pool.wait()
 
@@ -234,30 +244,43 @@
         "select": select, "gather": gather_chunk, "group": group_work,
         "near": relay_near, "far": relay_far,
     }
+    def ready():
+        for i in range(4):
+            for k in range(4):
+                if i or k:
+                    df, dx = fx_offset(i, k)
+                    device(f=df, x=dx)
+        for dz in (4, -4, 8):
+            device(z=dz)
+        get_targ.wait()
+
+    steps["ready"] = ready
     for name, *where in PLAN:
         steps[name](*where)
     pl.semaphore_wait(relay.at[1], 2)
 
-    def grad_of(slot):
-        part = slice(slot * 4 * ncen, (slot + 1) * 4 * ncen)
-        return jnp.dot(kern[part, :], resb[...], preferred_element_type=F32)
-
-    for i in range(4):
-        gq[i] = grad_of(other[i])
-        send(gq.at[i], gq_in.at[i], sgq.at[i], rgq.at[i], partner=True)
+    def grad_of(first):
+        rows = slice(first * group, (first + 1) * group)
+        both = jnp.dot(kern[rows, :], resb[...], preferred_element_type=F32)
+        return both.reshape(2, 4, ncen, outs)
+
+    for h in (0, 1):
+        part = slice(2 * h, 2 * h + 2)
+        gq[part] = grad_of(2 + h)
+        send(gq.at[part], gq_in.at[part], sgq.at[h], rgq.at[h], partner=True)
     total = []
-    for i in range(4):
-        mine = grad_of(own[i])
-        arrived(gq_in.at[i], rgq.at[i])
-        both = mine + gq_in[i]
-        total.append(both[0:ncen])
+    for h in (0, 1):
+        part = slice(2 * h, 2 * h + 2)
+        mine = grad_of(h)
+        arrived(gq_in.at[part], rgq.at[h])
+        both = mine + gq_in[part]
+        total += [both[0, 0], both[1, 0]]
         for j in (1, 2, 3):
-            gs[j, i] = both[j * ncen : (j + 1) * ncen].astype(BF16)
-        if i in (1, 3):
-            part = slice(i - 1, i + 1)
-            send(gs.at[3, part], gs_in.at[3, part], sgs.at[3, i], rgs.at[3], s=2 if i == 1 else -2)
-            for j in (1, 2):
-                send(gs.at[j, part], gs_in.at[NEG[j], part], sgs.at[j, i], rgs.at[NEG[j]], s=OFFS[j])
+            gs[j, part] = both[:, j].astype(BF16)
+        send(gs.at[3, part], gs_in.at[3, part], sgs.at[3, h], rgs.at[3], s=-2 if h else 2)
+        for j in (1, 2):
+            send(gs.at[j, part], gs_in.at[NEG[j], part], sgs.at[j, h], rgs.at[NEG[j]], s=OFFS[j])
+    sent()
     for j in (1, 2, 3):
         arrived(gs_in.at[j], rgs.at[j])
     eighth = ncen // NX
@@ -270,6 +293,7 @@
                 df, dx = fx_offset(i, k)
                 piece = lax.rem(here[0] + (dx + NX), NX)
                 send(gf.at[i, piece], gf_in.at[NEG[i], NEG[k]], sgf.at[i, k], rgf.at[NEG[i], NEG[k]], f=df, x=dx)
+    sent()
     mine = gf[0, here[0]]
     for i in range(4):
         for k in range(4):
@@ -280,6 +304,7 @@
     gz[...] = mine
     for k, dz in enumerate((4, -4, 8)):
         send(gz, gz_in.at[k], sgz.at[k], rgz.at[k], z=dz)
+    sent()
     for k in range(3):
         arrived(gz_in.at[k], rgz.at[k])
     out[here[0]] = (mine + gz_in[0]) + (gz_in[1] + gz_in[2])
@@ -289,8 +314,7 @@
         arrived(out.at[lax.rem(here[0] + (OFFS[k] + NX), NX)], rgx.at[k])
     grad_ref[...] = out[...].reshape(grad_ref.shape)
 
-    for copy in pending:
-        copy.wait_send()
+    sent()
 
 
 def per_device(point_pool, batch_rows, targets, center_pool, center_rows, coefs):
@@ -301,7 +325,6 @@
     vmem = pl.BlockSpec(memory_space=pltpu.VMEM)
     anys = pl.BlockSpec(memory_space=pl.ANY)
     dma = pltpu.SemaphoreType.DMA
-    half = 4 * ncen
     sub = ncen // NX
     scratch = [
         pltpu.VMEM((8, 4, ncen, d + outs), BF16),
@@ -315,8 +338,8 @@
         pltpu.VMEM(center_pool.shape, BF16),
         pltpu.VMEM((npts // 128, 128), jnp.int32),
         pltpu.VMEM((1, ncen), jnp.int32),
-        pltpu.VMEM((4, half, outs), F32),
-        pltpu.VMEM((4, half, outs), F32),
+        pltpu.VMEM((4, 4, ncen, outs), F32),
+        pltpu.VMEM((4, 4, ncen, outs), F32),
         pltpu.VMEM((4, 4, ncen, outs), BF16),
         pltpu.VMEM((4, 4, ncen, outs), BF16),
         pltpu.VMEM((4, NX, sub, outs), F32),

time: 55.7 us -> 55.7 us (level)
  no operation moved by 1% of the time
where the time goes in v5:
time: 55.7 us; the launch traced here: 55.6 us
  Pallas kernels  53.4 us (96%)
  local copies, waits for them, and re-layouts  1.59 us (3%)
  between operations  0.64 us (1%)
    pallas_call x1, Pallas kernels, per_device(): pl.pallas_call(kernel, out_shape=(jax.ShapeDtypeStruct((npts, outs), F32)...  53.4 us
    unnamed x2, local copies, waits for them, and re-layouts  1.59 us

profile of v5, /device:TPU:2, one launch (start us, length us, event | category | flops | bytes accessed | tf_op | source)
XLA Modules:
  0.0 55.6 jit_solution(15149655663662968867)
XLA Ops:
  0.6 53.4 %regression.1 = (f32[1024,256]{1,0:T(8,128)S(1)}, f32[32,256]{1,0:T(8,128)S(1)}) custom-call(bf16[1280,1024]{1,0:T(8,128)(2,1)} %pool_hbm.1, s32[8,128]{1,0:T(8,128)} %bitcast.2, bf16[1024,256]{1,0:T(8,128)(2,1)} %targ_hbm.1, bf16[64,1024]{1,0:T(8,128)(2,1)} %cpool_hbm.1, s32[1,32]{1,0:T(1,128)} %bitcast.3, bf16[32,256]{1,0:T(8,128)(2,1)} %coefs_hbm.1), custom_call_target="tpu_custom_call" | custom-call | tf_op jit(solution)/shard_map/regression/pallas_call | solution.py:354
  54.0 1.0 %copy.10 = f32[1024,256]{1,0:T(8,128)} copy(f32[1024,256]{1,0:T(8,128)S(1)} %get-tuple-element.4) | data formatting | bytes 2097152
  55.0 0.6 %copy.11 = f32[32,256]{1,0:T(8,128)} copy(f32[32,256]{1,0:T(8,128)S(1)} %get-tuple-element.5) | data formatting | bytes 65536

commit v6 on v5

--- a/solution.py
+++ b/solution.py
@@ -317,6 +317,17 @@
     sent()
 
 
+def put(res, grad, res_out, grad_out, sem):
+    copies = (
+        pltpu.make_async_copy(res, res_out, sem.at[0]),
+        pltpu.make_async_copy(grad, grad_out, sem.at[1]),
+    )
+    for copy in copies:
+        copy.start()
+    for copy in copies:
+        copy.wait()
+
+
 def per_device(point_pool, batch_rows, targets, center_pool, center_rows, coefs):
     batch_rows, center_rows = batch_rows.reshape(-1, 128), center_rows.reshape(1, -1)
     npool, d = point_pool.shape
@@ -351,7 +362,7 @@
         dma((4,)), dma((4,)), dma((4, 4)), dma((4,)), dma((4, 4)), dma((4, 4)),
         dma((3,)), dma((3,)), dma((4,)), dma((4,)), pltpu.SemaphoreType.REGULAR((2,)),
     ]
-    return pl.pallas_call(
+    held = pl.pallas_call(
         kernel,
         out_shape=(
             jax.ShapeDtypeStruct((npts, outs), F32),
@@ -368,6 +379,15 @@
         pltpu.with_memory_space_constraint(a, pltpu.HBM)
         for a in (point_pool, batch_rows, targets, center_pool, center_rows, coefs)
     ))
+    return pl.pallas_call(
+        put,
+        out_shape=tuple(jax.ShapeDtypeStruct(a.shape, a.dtype) for a in held),
+        in_specs=[anys] * 2,
+        out_specs=(anys, anys),
+        scratch_shapes=[dma((2,))],
+        compiler_params=pltpu.CompilerParams(vmem_limit_bytes=1 << 20),
+        name="put",
+    )(*held)
 
 
 def solution(mesh):

time: 55.7 us -> 55.1 us (0.989)
  local copies, waits for them, and re-layouts: 1.59 us -> 0 us
  Pallas kernels: 53.4 us -> 54.4 us
    unnamed x2 -> x0, local copies, waits for them, and re-layouts: 1.59 us -> none
    pallas_call x0 -> x1, Pallas kernels: none -> 0.99 us  [per_device(): pl.pallas_call(put, out_shape=tuple((jax.ShapeDtypeStruct(a.shape, a.dtyp...]
where the time goes in v6:
time: 55.1 us; the launch traced here: 55 us
  Pallas kernels  54.4 us (99%)
  between operations  0.64 us (1%)
    pallas_call x1, Pallas kernels, per_device(): pl.pallas_call(kernel, out_shape=(jax.ShapeDtypeStruct((npts, outs), F32)...  53.4 us

profile of v6, /device:TPU:2, one launch (start us, length us, event | category | flops | bytes accessed | tf_op | source)
XLA Modules:
  0.0 55.0 jit_solution(3683290192103752457)
XLA Ops:
  0.6 53.4 %regression.1 = (f32[1024,256]{1,0:T(8,128)S(1)}, f32[32,256]{1,0:T(8,128)S(1)}) custom-call(bf16[1280,1024]{1,0:T(8,128)(2,1)} %pool_hbm.1, s32[8,128]{1,0:T(8,128)} %bitcast.2, bf16[1024,256]{1,0:T(8,128)(2,1)} %targ_hbm.1, bf16[64,1024]{1,0:T(8,128)(2,1)} %cpool_hbm.1, s32[1,32]{1,0:T(1,128)} %bitcast.3, bf16[32,256]{1,0:T(8,128)(2,1)} %coefs_hbm.1), custom_call_target="tpu_custom_call" | custom-call | tf_op jit(solution)/shard_map/regression/pallas_call | solution.py:365
  54.0 1.0 %put.1 = (f32[1024,256]{1,0:T(8,128)}, f32[32,256]{1,0:T(8,128)}) custom-call(f32[1024,256]{1,0:T(8,128)S(1)} %get-tuple-element.4.res, f32[32,256]{1,0:T(8,128)S(1)} %get-tuple-element.5.grad), custom_call_target="tpu_custom_call" | custom-call | tf_op jit(solution)/shard_map/put/pallas_call | solution.py:382

commit v7 on v6

--- a/solution.py
+++ b/solution.py
@@ -266,14 +266,14 @@
 
     for h in (0, 1):
         part = slice(2 * h, 2 * h + 2)
-        gq[part] = grad_of(2 + h)
+        gq[part] = grad_of(2 + h).astype(BF16)
         send(gq.at[part], gq_in.at[part], sgq.at[h], rgq.at[h], partner=True)
     total = []
     for h in (0, 1):
         part = slice(2 * h, 2 * h + 2)
         mine = grad_of(h)
         arrived(gq_in.at[part], rgq.at[h])
-        both = mine + gq_in[part]
+        both = mine + gq_in[part].astype(F32)
         total += [both[0, 0], both[1, 0]]
         for j in (1, 2, 3):
             gs[j, part] = both[:, j].astype(BF16)
@@ -301,13 +301,14 @@
                 arrived(gf_in.at[i, k], rgf.at[i, k])
                 mine = mine + gf_in[i, k]
 
-    gz[...] = mine
+    gz[...] = mine.astype(BF16)
     for k, dz in enumerate((4, -4, 8)):
         send(gz, gz_in.at[k], sgz.at[k], rgz.at[k], z=dz)
     sent()
     for k in range(3):
         arrived(gz_in.at[k], rgz.at[k])
-    out[here[0]] = (mine + gz_in[0]) + (gz_in[1] + gz_in[2])
+    mine = gz[...].astype(F32)
+    out[here[0]] = mine + (gz_in[0].astype(F32) + (gz_in[1].astype(F32) + gz_in[2].astype(F32)))
     for k in (3, 1, 2):
         send(out.at[here[0]], out.at[here[0]], sgx.at[k], rgx.at[NEG[k]], x=OFFS[k])
     for k in (1, 2, 3):
@@ -349,14 +350,14 @@
         pltpu.VMEM(center_pool.shape, BF16),
         pltpu.VMEM((npts // 128, 128), jnp.int32),
         pltpu.VMEM((1, ncen), jnp.int32),
-        pltpu.VMEM((4, 4, ncen, outs), F32),
-        pltpu.VMEM((4, 4, ncen, outs), F32),
+        pltpu.VMEM((4, 4, ncen, outs), BF16),
+        pltpu.VMEM((4, 4, ncen, outs), BF16),
         pltpu.VMEM((4, 4, ncen, outs), BF16),
         pltpu.VMEM((4, 4, ncen, outs), BF16),
         pltpu.VMEM((4, NX, sub, outs), F32),
         pltpu.VMEM((4, NX, sub, outs), F32),
-        pltpu.VMEM((sub, outs), F32),
-        pltpu.VMEM((3, sub, outs), F32),
+        pltpu.VMEM((sub, outs), BF16),
+        pltpu.VMEM((3, sub, outs), BF16),
         pltpu.VMEM((NX, sub, outs), F32),
         dma((6,)), dma((4,)), dma((4, 4)), dma((4, 4)), dma((4, 4)), dma((4, 4)),
         dma((4,)), dma((4,)), dma((4, 4)), dma((4,)), dma((4, 4)), dma((4, 4)),

time: 55.1 us -> 54.8 us (level)
  no operation moved by 1% of the time
where the time goes in v7:
time: 54.8 us; the launch traced here: 54.7 us
  Pallas kernels  54.1 us (99%)
  between operations  0.64 us (1%)
    pallas_call x1, Pallas kernels, per_device(): pl.pallas_call(kernel, out_shape=(jax.ShapeDtypeStruct((npts, outs), F32)...  53.1 us

profile of v7, /device:TPU:2, one launch (start us, length us, event | category | flops | bytes accessed | tf_op | source)
XLA Modules:
  0.0 54.7 jit_solution(2413873953694834554)
XLA Ops:
  0.6 53.1 %regression.1 = (f32[1024,256]{1,0:T(8,128)S(1)}, f32[32,256]{1,0:T(8,128)S(1)}) custom-call(bf16[1280,1024]{1,0:T(8,128)(2,1)} %pool_hbm.1, s32[8,128]{1,0:T(8,128)} %bitcast.2, bf16[1024,256]{1,0:T(8,128)(2,1)} %targ_hbm.1, bf16[64,1024]{1,0:T(8,128)(2,1)} %cpool_hbm.1, s32[1,32]{1,0:T(1,128)} %bitcast.3, bf16[32,256]{1,0:T(8,128)(2,1)} %coefs_hbm.1), custom_call_target="tpu_custom_call" | custom-call | tf_op jit(solution)/shard_map/regression/pallas_call | solution.py:366
  53.7 1.0 %put.1 = (f32[1024,256]{1,0:T(8,128)}, f32[32,256]{1,0:T(8,128)}) custom-call(f32[1024,256]{1,0:T(8,128)S(1)} %get-tuple-element.4.res, f32[32,256]{1,0:T(8,128)S(1)} %get-tuple-element.5.grad), custom_call_target="tpu_custom_call" | custom-call | tf_op jit(solution)/shard_map/put/pallas_call | solution.py:383

commit v8 on v6

--- a/solution.py
+++ b/solution.py
@@ -266,14 +266,14 @@
 
     for h in (0, 1):
         part = slice(2 * h, 2 * h + 2)
-        gq[part] = grad_of(2 + h)
+        gq[part] = grad_of(2 + h).astype(BF16)
         send(gq.at[part], gq_in.at[part], sgq.at[h], rgq.at[h], partner=True)
     total = []
     for h in (0, 1):
         part = slice(2 * h, 2 * h + 2)
         mine = grad_of(h)
         arrived(gq_in.at[part], rgq.at[h])
-        both = mine + gq_in[part]
+        both = mine + gq_in[part].astype(F32)
         total += [both[0, 0], both[1, 0]]
         for j in (1, 2, 3):
             gs[j, part] = both[:, j].astype(BF16)
@@ -349,8 +349,8 @@
         pltpu.VMEM(center_pool.shape, BF16),
         pltpu.VMEM((npts // 128, 128), jnp.int32),
         pltpu.VMEM((1, ncen), jnp.int32),
-        pltpu.VMEM((4, 4, ncen, outs), F32),
-        pltpu.VMEM((4, 4, ncen, outs), F32),
+        pltpu.VMEM((4, 4, ncen, outs), BF16),
+        pltpu.VMEM((4, 4, ncen, outs), BF16),
         pltpu.VMEM((4, 4, ncen, outs), BF16),
         pltpu.VMEM((4, 4, ncen, outs), BF16),
         pltpu.VMEM((4, NX, sub, outs), F32),

time: 55.1 us -> 55 us (level)
  no operation moved by 1% of the time
where the time goes in v8:
time: 55 us; the launch traced here: 54.9 us
  Pallas kernels  54.2 us (99%)
  between operations  0.64 us (1%)
    pallas_call x1, Pallas kernels, per_device(): pl.pallas_call(kernel, out_shape=(jax.ShapeDtypeStruct((npts, outs), F32)...  53.2 us

profile of v8, /device:TPU:2, one launch (start us, length us, event | category | flops | bytes accessed | tf_op | source)
XLA Modules:
  0.0 54.9 jit_solution(3166792083377550096)
XLA Ops:
  0.6 53.2 %regression.1 = (f32[1024,256]{1,0:T(8,128)S(1)}, f32[32,256]{1,0:T(8,128)S(1)}) custom-call(bf16[1280,1024]{1,0:T(8,128)(2,1)} %pool_hbm.1, s32[8,128]{1,0:T(8,128)} %bitcast.2, bf16[1024,256]{1,0:T(8,128)(2,1)} %targ_hbm.1, bf16[64,1024]{1,0:T(8,128)(2,1)} %cpool_hbm.1, s32[1,32]{1,0:T(1,128)} %bitcast.3, bf16[32,256]{1,0:T(8,128)(2,1)} %coefs_hbm.1), custom_call_target="tpu_custom_call" | custom-call | tf_op jit(solution)/shard_map/regression/pallas_call | solution.py:365
  53.9 1.0 %put.1 = (f32[1024,256]{1,0:T(8,128)}, f32[32,256]{1,0:T(8,128)}) custom-call(f32[1024,256]{1,0:T(8,128)S(1)} %get-tuple-element.4.res, f32[32,256]{1,0:T(8,128)S(1)} %get-tuple-element.5.grad), custom_call_target="tpu_custom_call" | custom-call | tf_op jit(solution)/shard_map/put/pallas_call | solution.py:382
